TPU v7x, 128 devices: a whole 4x4x4 slice. The times are simulated.
128 devices in a mesh: row: 8 (over y_lo, z), col: 16 (over x, y_hi, core).
Axes of the slice: x: 4, y: 4 (y_hi: 2, y_lo: 2; y = y_hi * 2 + y_lo), z: 4, core: 2. Of those that a mesh axis runs over, the one named last changes fastest.
Arguments:
- feats_one: bfloat16 [65536, 256], P(('row', 'col')), may hold values from -6 to 6
- feats_two: bfloat16 [65536, 256], P(('row', 'col')), may hold values from -6 to 6
- target_view: bfloat16 [65536, 256], P(('row', 'col')), may hold values from -6 to 6
- negatives: int32 [65536], P(('row', 'col')), may hold values from 0 to 511
- weight_one: bfloat16 [256, 256], replicated, may hold values from -0.375 to 0.375
- weight_two: bfloat16 [256, 256], replicated, may hold values from -0.375 to 0.375
- block_tiles: bfloat16 [81920, 128, 128], P(('row', 'col')), may hold values from -0.15625 to 0.15625
- tile_rows: int32 [81920], P(('row', 'col')), may hold values from 0 to 31
- tile_cols: int32 [81920], P(('row', 'col')), may hold values from 0 to 31
- block_counts: int32 [128], P(('row', 'col')), may hold values from 80 to 640, as said below
- need_rows: int32 [128, 16, 2], P(('row', 'col')), may hold values from 0 to 3, as said below
Outputs:
- grad_hidden: bfloat16 [65536, 256], P(('row', 'col'))
- grad_first: float32 [256, 256], replicated
- grad_second: float32 [256, 256], replicated
Inputs may be any that keep to these rules, and one draw needn't show every extreme that they name: `need_rows`: for each owner and source, the 2 entries are distinct. `block_counts`: live tiles of one block list.
All inputs are finite; a program needn't handle non-finite values.
Results may differ from a plain program's by a relative error of at most 0.0063.
Values may be sent and summed in bfloat16 or wider, within the bound.
No kernel may reach another device: no remote copies, remote signals or barrier semaphores. Data moves between devices by JAX's collectives and lax.ppermute only.
A program may use at most 192 MiB of HBM per device.

v0:
```python
import math

import jax
import jax.numpy as jnp
from jax import lax
from jax.sharding import PartitionSpec as P


def silu_slope(values):
    sig = jax.nn.sigmoid(values)
    return sig * (1.0 + values * (1.0 - sig))


def column_product(left, right):
    return lax.dot_general(
        left, right, (((0,), (0,)), ((), ())), preferred_element_type=jnp.float32
    )


def on_device(
    feats_one,
    feats_two,
    target_view,
    negatives,
    weight_one,
    weight_two,
    block_tiles,
    tile_rows,
    tile_cols,
    block_counts,
    need_rows,
):
    node_dev, features = feats_two.shape
    capacity, tile_size = (block_tiles.shape[0], block_tiles.shape[1])
    sources = lax.axis_size("col")
    row_group = lax.axis_size("row")
    tiles_dev = node_dev // tile_size
    slot_count = need_rows.shape[2]
    col_count = row_group * tiles_dev
    inverse_root = 1.0 / math.sqrt(features)
    weight_norm = 1.0 / math.sqrt(node_dev * row_group * sources)
    pre_two = jnp.dot(feats_two, weight_two, preferred_element_type=jnp.float32)
    hidden = jax.nn.silu(pre_two)
    partner_rows = hidden[negatives]
    target_full = target_view.astype(jnp.float32)
    s_pos = jnp.sum(hidden * target_full, axis=-1) * inverse_root
    s_neg = jnp.sum(hidden * partner_rows, axis=-1) * inverse_root
    prob_pos = jax.nn.sigmoid(-s_pos)
    prob_neg = jax.nn.sigmoid(s_neg)
    grad_out = -prob_pos[:, None] * target_full + prob_neg[:, None] * partner_rows
    grad_out = grad_out + jax.ops.segment_sum(
        prob_neg[:, None] * hidden, negatives, num_segments=node_dev
    )
    dpre_two = (grad_out * silu_slope(pre_two)).astype(jnp.bfloat16)
    grad_second = column_product(feats_two, dpre_two)
    grad_second = lax.psum(grad_second, ("row", "col"))
    message = lax.dot_general(
        dpre_two, weight_two, (((1,), (1,)), ((), ())), preferred_element_type=jnp.float32
    ).astype(jnp.bfloat16)
    gathered = lax.all_gather(message, "col", axis=0, tiled=True)
    buffer_tiles = gathered.reshape(sources * tiles_dev, tile_size, features)
    need_flat = need_rows[0].reshape(-1)
    slot_ids = jnp.arange(sources * slot_count, dtype=jnp.int32)
    local_tile = jnp.sum(
        jnp.where(tile_rows[:, None] == slot_ids[None, :], need_flat[None, :], 0), axis=1
    )
    row_tile = tile_rows // slot_count * tiles_dev + local_tile
    block_len = 128
    rounds = capacity // block_len
    live = (jnp.arange(capacity, dtype=jnp.int32) < block_counts[0]).astype(jnp.float32)
    column_ids = jnp.arange(col_count, dtype=jnp.int32)

    def add_block(summed_tiles, pieces):
        tile_part, row_part, col_part, live_part = pieces
        gathered_rows = buffer_tiles[row_part]
        contrib = jnp.einsum(
            "ktu,ktf->kuf", tile_part, gathered_rows, preferred_element_type=jnp.float32
        )
        selector = jnp.where(col_part[:, None] == column_ids[None, :], live_part[:, None], 0.0)
        placed = jnp.einsum(
            "kc,kuf->cuf",
            selector,
            contrib,
            precision=lax.Precision.HIGHEST,
            preferred_element_type=jnp.float32,
        )
        return (summed_tiles + placed, None)

    start_tiles = jnp.zeros((col_count, tile_size, features), jnp.float32)
    summed_tiles, _ = lax.scan(
        add_block,
        start_tiles,
        (
            block_tiles.reshape(rounds, block_len, tile_size, tile_size),
            row_tile.reshape(rounds, block_len),
            tile_cols.reshape(rounds, block_len),
            live.reshape(rounds, block_len),
        ),
    )
    column_total = lax.psum_scatter(
        summed_tiles.reshape(col_count * tile_size, features),
        "row",
        scatter_dimension=0,
        tiled=True,
    )
    grad_hidden = column_total.astype(jnp.bfloat16)
    pre_one = jnp.dot(feats_one, weight_one, preferred_element_type=jnp.float32)
    dpre_one = (grad_hidden.astype(jnp.float32) * silu_slope(pre_one)).astype(jnp.bfloat16)
    grad_first = column_product(feats_one, dpre_one)
    grad_first = lax.psum(grad_first, ("row", "col"))
    return (grad_hidden, grad_first * weight_norm, grad_second * weight_norm)


def solution(mesh):
    return jax.shard_map(
        on_device,
        mesh=mesh,
        in_specs=(
            P(("row", "col"), None),
            P(("row", "col"), None),
            P(("row", "col"), None),
            P(("row", "col")),
            P(),
            P(),
            P(("row", "col"), None, None),
            P(("row", "col")),
            P(("row", "col")),
            P(("row", "col")),
            P(("row", "col"), None, None),
        ),
        out_specs=(P(("row", "col"), None), P(), P()),
        check_vma=False,
    )
```

profile of v0, /device:TPU:1, one launch (start us, length us, event | category | flops | bytes accessed | tf_op | source)
XLA Modules:
  0.0 544.6 jit_solution(12721467284938459450)
XLA Ops:
  7.2 1.0 copy-done
  8.2 1.2 fusion.22
  10.4 1.6 gather_fusion.1
  13.1 3.5 scatter_fusion
  17.0 1.0 convolution_convert_fusion
  18.1 27.9 %copy.40 = bf16[640,128,128]{1,2,0:T(8,128)(2,1)} copy(bf16[640,128,128]{2,1,0:T(8,128)(2,1)} %param.19) | data formatting | bytes 41943040 | tf_op args[6]
  47.0 30.8 %all-gather.2.cloned.1.call-done = bf16[8192,256]{1,0:T(8,128)(2,1)} async-done(((bf16[512,256]{1,0:T(8,128)(2,1)}), bf16[8192,256]{1,0:T(8,128)(2,1)}) %all-gather.2.cloned.1.call-update) | async-done | bytes 4194320 | tf_op jit(solution)/shard_map/all_gather | solution.py:60
  77.8 241.0 %while.11 = (s32[]{:T(128)}, f32[32,128,256]{2,0,1:T(8,128)}, s32[5,128]{1,0:T(8,128)}, f32[5,128]{1,0:T(8,128)S(1)}, bf16[5,128,128,128]{2,3,1,0:T(8,128)(2,1)}...) while((s32[]{:T(128)}, f32[32,128,256]{2,0,1:T(8,128)}, ...), condition=%wide.region_5.6_spmd.clone, body=%wide.region_4.5_spmd.clone.sunk | while | flops 2686461440 | bytes 71313008 | solution.py:90
  77.8 8.7 %gather_fusion = bf16[128,128,256]{2,1,0:T(8,128)(2,1)} fusion(bf16[64,128,256]{2,1,0:T(8,128)(2,1)} %get-tuple-element.172, s32[1024]{0:T(1024)S(1)} %pad_clamp_fusion.3), kind=kCustom, calls=%fused_computation.clone.clone.1 | custom fusion | bytes 16777728 | tf_op jit(solution)/shard_map/while/body/eval_jaxpr/gather | solution.py:75
  86.6 12.8 %fusion.55 = f32[128,128,256]{2,1,0:T(8,128)} fusion(bf16[128,128,256]{2,1,0:T(8,128)(2,1)} %gather_fusion, bf16[5,128,128,128]{2,3,1,0:T(8,128)(2,1)} %get-tuple-element.170, s32[]{:T(128)} %get-tuple-element.157), kind=kOutput, calls=%fused_computation.6.clone.1 | convolution fusion | flops 1073741824 | bytes 29360640 | tf_op jit(solution)/shard_map/while/body/eval_jaxpr/ktu,ktf->kuf/dot_general | solution.py:76
  100.1 25.4 %select_add_fusion.2 = f32[32,128,256]{2,0,1:T(8,128)} fusion(f32[32,128,256]{2,0,1:T(8,128)} %get-tuple-element.158, pred[]{:T(512)S(6)} %compare.5, f32[128,128,256]{2,1,0:T(8,128)} %fusion.55, f32[128]{0:T(128)S(1)} %fusion.56, s32[128]{0:T(128)S(1)} %fusion.57), kind=kOutput, calls=%fused_computation.8.clone.1 | convolution fusion | flops 1612718080 | bytes 25166848 | tf_op jit(solution)/shard_map/while/body/eval_jaxpr/kc,kuf->cuf/dot_general | solution.py:80
  125.6 8.7 %gather_fusion = bf16[128,128,256]{2,1,0:T(8,128)(2,1)} fusion(bf16[64,128,256]{2,1,0:T(8,128)(2,1)} %get-tuple-element.172, s32[1024]{0:T(1024)S(1)} %pad_clamp_fusion.3), kind=kCustom, calls=%fused_computation.clone.clone.1 | custom fusion | bytes 16777728 | tf_op jit(solution)/shard_map/while/body/eval_jaxpr/gather | solution.py:75
  134.3 12.8 %fusion.55 = f32[128,128,256]{2,1,0:T(8,128)} fusion(bf16[128,128,256]{2,1,0:T(8,128)(2,1)} %gather_fusion, bf16[5,128,128,128]{2,3,1,0:T(8,128)(2,1)} %get-tuple-element.170, s32[]{:T(128)} %get-tuple-element.157), kind=kOutput, calls=%fused_computation.6.clone.1 | convolution fusion | flops 1073741824 | bytes 29360640 | tf_op jit(solution)/shard_map/while/body/eval_jaxpr/ktu,ktf->kuf/dot_general | solution.py:76
  147.8 26.0 %select_add_fusion.2 = f32[32,128,256]{2,0,1:T(8,128)} fusion(f32[32,128,256]{2,0,1:T(8,128)} %get-tuple-element.158, pred[]{:T(512)S(6)} %compare.5, f32[128,128,256]{2,1,0:T(8,128)} %fusion.55, f32[128]{0:T(128)S(1)} %fusion.56, s32[128]{0:T(128)S(1)} %fusion.57), kind=kOutput, calls=%fused_computation.8.clone.1 | convolution fusion | flops 1612718080 | bytes 25166848 | tf_op jit(solution)/shard_map/while/body/eval_jaxpr/kc,kuf->cuf/dot_general | solution.py:80
  173.9 8.7 %gather_fusion = bf16[128,128,256]{2,1,0:T(8,128)(2,1)} fusion(bf16[64,128,256]{2,1,0:T(8,128)(2,1)} %get-tuple-element.172, s32[1024]{0:T(1024)S(1)} %pad_clamp_fusion.3), kind=kCustom, calls=%fused_computation.clone.clone.1 | custom fusion | bytes 16777728 | tf_op jit(solution)/shard_map/while/body/eval_jaxpr/gather | solution.py:75
  182.6 12.8 %fusion.55 = f32[128,128,256]{2,1,0:T(8,128)} fusion(bf16[128,128,256]{2,1,0:T(8,128)(2,1)} %gather_fusion, bf16[5,128,128,128]{2,3,1,0:T(8,128)(2,1)} %get-tuple-element.170, s32[]{:T(128)} %get-tuple-element.157), kind=kOutput, calls=%fused_computation.6.clone.1 | convolution fusion | flops 1073741824 | bytes 29360640 | tf_op jit(solution)/shard_map/while/body/eval_jaxpr/ktu,ktf->kuf/dot_general | solution.py:76
  196.2 26.0 %select_add_fusion.2 = f32[32,128,256]{2,0,1:T(8,128)} fusion(f32[32,128,256]{2,0,1:T(8,128)} %get-tuple-element.158, pred[]{:T(512)S(6)} %compare.5, f32[128,128,256]{2,1,0:T(8,128)} %fusion.55, f32[128]{0:T(128)S(1)} %fusion.56, s32[128]{0:T(128)S(1)} %fusion.57), kind=kOutput, calls=%fused_computation.8.clone.1 | convolution fusion | flops 1612718080 | bytes 25166848 | tf_op jit(solution)/shard_map/while/body/eval_jaxpr/kc,kuf->cuf/dot_general | solution.py:80
  222.2 8.7 %gather_fusion = bf16[128,128,256]{2,1,0:T(8,128)(2,1)} fusion(bf16[64,128,256]{2,1,0:T(8,128)(2,1)} %get-tuple-element.172, s32[1024]{0:T(1024)S(1)} %pad_clamp_fusion.3), kind=kCustom, calls=%fused_computation.clone.clone.1 | custom fusion | bytes 16777728 | tf_op jit(solution)/shard_map/while/body/eval_jaxpr/gather | solution.py:75
  230.9 12.8 %fusion.55 = f32[128,128,256]{2,1,0:T(8,128)} fusion(bf16[128,128,256]{2,1,0:T(8,128)(2,1)} %gather_fusion, bf16[5,128,128,128]{2,3,1,0:T(8,128)(2,1)} %get-tuple-element.170, s32[]{:T(128)} %get-tuple-element.157), kind=kOutput, calls=%fused_computation.6.clone.1 | convolution fusion | flops 1073741824 | bytes 29360640 | tf_op jit(solution)/shard_map/while/body/eval_jaxpr/ktu,ktf->kuf/dot_general | solution.py:76
  244.5 26.0 %select_add_fusion.2 = f32[32,128,256]{2,0,1:T(8,128)} fusion(f32[32,128,256]{2,0,1:T(8,128)} %get-tuple-element.158, pred[]{:T(512)S(6)} %compare.5, f32[128,128,256]{2,1,0:T(8,128)} %fusion.55, f32[128]{0:T(128)S(1)} %fusion.56, s32[128]{0:T(128)S(1)} %fusion.57), kind=kOutput, calls=%fused_computation.8.clone.1 | convolution fusion | flops 1612718080 | bytes 25166848 | tf_op jit(solution)/shard_map/while/body/eval_jaxpr/kc,kuf->cuf/dot_general | solution.py:80
  270.5 8.7 %gather_fusion = bf16[128,128,256]{2,1,0:T(8,128)(2,1)} fusion(bf16[64,128,256]{2,1,0:T(8,128)(2,1)} %get-tuple-element.172, s32[1024]{0:T(1024)S(1)} %pad_clamp_fusion.3), kind=kCustom, calls=%fused_computation.clone.clone.1 | custom fusion | bytes 16777728 | tf_op jit(solution)/shard_map/while/body/eval_jaxpr/gather | solution.py:75
  279.3 12.8 %fusion.55 = f32[128,128,256]{2,1,0:T(8,128)} fusion(bf16[128,128,256]{2,1,0:T(8,128)(2,1)} %gather_fusion, bf16[5,128,128,128]{2,3,1,0:T(8,128)(2,1)} %get-tuple-element.170, s32[]{:T(128)} %get-tuple-element.157), kind=kOutput, calls=%fused_computation.6.clone.1 | convolution fusion | flops 1073741824 | bytes 29360640 | tf_op jit(solution)/shard_map/while/body/eval_jaxpr/ktu,ktf->kuf/dot_general | solution.py:76
  292.8 26.0 %select_add_fusion.2 = f32[32,128,256]{2,0,1:T(8,128)} fusion(f32[32,128,256]{2,0,1:T(8,128)} %get-tuple-element.158, pred[]{:T(512)S(6)} %compare.5, f32[128,128,256]{2,1,0:T(8,128)} %fusion.55, f32[128]{0:T(128)S(1)} %fusion.56, s32[128]{0:T(128)S(1)} %fusion.57), kind=kOutput, calls=%fused_computation.8.clone.1 | convolution fusion | flops 1612718080 | bytes 25166848 | tf_op jit(solution)/shard_map/while/body/eval_jaxpr/kc,kuf->cuf/dot_general | solution.py:80
  318.8 5.9 %copy.49 = f32[32,128,256]{1,0,2:T(8,128)} copy(f32[32,128,256]{2,0,1:T(8,128)} %get-tuple-element.45) | data formatting | bytes 8388608 | tf_op jit(solution)/shard_map/while | solution.py:90
  324.8 8.0 %copy.62 = f32[32,8,32,128]{3,1,2,0:T(8,128)} copy(f32[32,8,32,128]{3,2,1,0:T(8,128)} %bitcast.62) | data formatting | bytes 8388608
  332.9 0.9 convolution_bitcast_fusion
  333.8 50.9 %reduce-scatter.2.cloned.1.call-done = f32[512,256]{0,1:T(8,128)} async-done(((f32[4096,256]{0,1:T(8,128)}), f32[512,256]{0,1:T(8,128)}) %reduce-scatter.2.cloned.1.call-update) | async-done | bytes 524304 | tf_op jit(solution)/shard_map/reduce_scatter | solution.py:100
  384.7 1.1 convert_element_type.26
  385.8 1.2 convolution_bitcast_fusion.1
  387.9 146.5 %all-reduce.3.cloned.1.call-done = (f32[256,256]{0,1:T(8,128)}, f32[256,256]{0,1:T(8,128)}) async-done(((f32[256,256]{0,1:T(8,128)}, f32[256,256]{0,1:T(8,128)}), (f32[256,256]{0,1:T(8,128)}, f32[256,256]{0,1:T(8,128)})) %all-reduce.3.cloned.1.call-update) | async-done | bytes 524304 | tf_op jit(solution)/shard_map/psum | solution.py:110
  534.4 1.0 broadcast_multiply_fusion.2
  536.2 1.0 broadcast_multiply_fusion.1
  (62 shorter events, 8.9 us)
Async XLA Ops:
  7.2 1.0 copy-start
  7.2 5.9 %copy-start.4 = (s32[512]{0:T(512)S(1)}, s32[512]{0:T(512)}, u32[]{:S(2)}) copy-start(s32[512]{0:T(512)} %param.16) | copy-start | bytes 6148
  7.2 4.9 copy-start.1
  7.2 70.6 %all-gather.2.cloned.1.call-start = ((), (), s32[]{:S(2)}) async-start(), calls=%async_computation.1 | async-start | bytes 4456448 | tf_op jit(solution)/shard_map/all_gather | solution.py:60
  12.3 4.7 copy-start.2
  18.0 366.7 %reduce-scatter.2.cloned.1.call-start = ((), (), s32[]{:S(2)}) async-start(), calls=%async_computation.2 | async-start | bytes 4718592 | tf_op jit(solution)/shard_map/reduce_scatter | solution.py:100
  18.1 27.9 %copy-start.5 = (s32[1,16,2]{1,2,0:T(2,128)S(1)}, s32[1,16,2]{1,2,0:T(2,128)}, u32[]{:S(2)}) copy-start(s32[1,16,2]{1,2,0:T(2,128)} %param.23) | copy-start | bytes 388
  18.1 28.8 %copy-start.3 = (s32[640]{0:T(1024)S(1)}, s32[640]{0:T(1024)}, u32[]{:S(2)}) copy-start(s32[640]{0:T(1024)} %param.20) | copy-start | bytes 7684
  324.8 61.0 %copy-start.6 = (bf16[512,256]{1,0:T(8,128)(2,1)S(1)}, bf16[512,256]{1,0:T(8,128)(2,1)}, u32[]{:S(2)}) copy-start(bf16[512,256]{1,0:T(8,128)(2,1)} %param.13) | copy-start | bytes 786436
  324.8 61.0 %copy-start.7 = (bf16[256,256]{1,0:T(8,128)(2,1)S(1)}, bf16[256,256]{1,0:T(8,128)(2,1)}, u32[]{:S(2)}) copy-start(bf16[256,256]{1,0:T(8,128)(2,1)} %param.17) | copy-start | bytes 393220
  332.8 201.6 %all-reduce.3.cloned.1.call-start = ((), (), s32[]{:S(2)}) async-start(), calls=%async_computation.3 | async-start | bytes 1048576 | tf_op jit(solution)/shard_map/psum | solution.py:110
Sparse Core Ops, SparseCore 0:
  18.2 59.5 all-gather.1
  332.9 51.7 reduce-scatter.1
  390.3 144.1 all-reduce.2
where the time goes:
time: 546 us; the launch traced here: 545 us
  waiting for transfers between devices  228 us (42%)
  matrix products  198 us (36%)
  local copies, waits for them, and re-layouts  95.4 us (17%)
  between operations  14.6 us (3%)
  other arithmetic  7.94 us (1%)
    psum x1, waiting for transfers between devices, on_device(): grad_first = lax.psum(grad_first, ('row', 'col'))  147 us
    dot_general x5, matrix products, add_block(): jnp.einsum('kc,kuf->cuf', selector, contrib, precision=lax.Precision.HIGH...  130 us
    dot_general x5, matrix products, add_block(): jnp.einsum('ktu,ktf->kuf', tile_part, gathered_rows, preferred_element_ty...  64.1 us
    reduce_scatter x1, waiting for transfers between devices, on_device(): lax.psum_scatter(summed_tiles.reshape(col_count * tile_size, features), '...  50.9 us
    gather x5, local copies, waits for them, and re-layouts, add_block(): gathered_rows = buffer_tiles[row_part]  43.7 us
    unnamed x23, local copies, waits for them, and re-layouts  39.7 us
    all_gather x1, waiting for transfers between devices, on_device(): gathered = lax.all_gather(message, 'col', axis=0, tiled=True)  30.8 us
  transfers between devices with their start and end apart: 3, of which 3 were waited for; matrix products, arithmetic and copies ran while one was open for 6% of the time, Pallas kernels for 0%

commit v1 on v0

v1 whole, which is shorter than its diff:
```python
import math

import jax
import jax.numpy as jnp
from jax import lax
from jax.experimental import pallas as pl
from jax.experimental.pallas import tpu as pltpu
from jax.sharding import PartitionSpec as P

F32 = jnp.float32
BF16 = jnp.bfloat16
CHUNK = 16
RING = 4


def sigmoid(values):
    return jax.nn.sigmoid(values)


def dot(left, right, left_dim, right_dim):
    return lax.dot_general(
        left, right, (((left_dim,), (right_dim,)), ((), ())), preferred_element_type=F32
    )


def split(values):
    high = values.astype(BF16)
    low = (values - high.astype(F32)).astype(BF16)
    return jnp.concatenate([high, low], axis=1)


def message_kernel(
    need_ref, feats_ref, target_ref, negatives_ref, weight_ref, send_ref, grad_ref, message_ref
):
    nodes, features = feats_ref.shape
    tiles, tile_size, _ = message_ref.shape
    inverse_root = 1.0 / math.sqrt(features)
    feats = feats_ref[...]
    weight = weight_ref[...]
    pre = dot(feats, weight, 1, 0)
    sig = sigmoid(pre)
    hidden = pre * sig
    ids = lax.broadcasted_iota(jnp.int32, (nodes, nodes), 0)
    picks = jnp.where(ids == negatives_ref[...], 1.0, 0.0).astype(BF16)
    both = dot(picks, split(hidden), 0, 0)
    partner = both[:, :features] + both[:, features:]
    target = target_ref[...].astype(F32)
    s_pos = jnp.sum(hidden * target, axis=-1, keepdims=True) * inverse_root
    s_neg = jnp.sum(hidden * partner, axis=-1, keepdims=True) * inverse_root
    prob_pos = sigmoid(-s_pos)
    prob_neg = sigmoid(s_neg)
    both = dot(picks, split(prob_neg * hidden), 1, 0)
    grad_out = prob_neg * partner - prob_pos * target + both[:, :features] + both[:, features:]
    dpre = (grad_out * (sig * (1.0 + pre * (1.0 - sig)))).astype(BF16)
    message = dot(dpre, weight, 1, 1).astype(BF16)
    message_ref[...] = message.reshape(tiles, tile_size, features)
    grad_ref[...] = dot(feats, dpre, 0, 0)

    for slot in range(send_ref.shape[0]):
        send_ref[slot] = message_ref[need_ref[slot]]


def product_kernel(
    rows_ref, cols_ref, count_ref, tiles_ref, received_ref, out_ref, sums_ref, buffer_ref, sems
):
    col_tiles = out_ref.shape[0]
    count = count_ref[0]
    chunks = (count + CHUNK - 1) // CHUNK

    def fetch(chunk):
        slot = lax.rem(chunk, RING)
        return pltpu.make_async_copy(
            tiles_ref.at[pl.ds(chunk * CHUNK, CHUNK)], buffer_ref.at[slot], sems.at[slot]
        )

    for ahead in range(RING - 1):

        @pl.when(ahead < chunks)
        def _():
            fetch(jnp.int32(ahead)).start()

    sums_ref[...] = jnp.zeros(sums_ref.shape, F32)

    def step(chunk, carry):
        @pl.when(chunk + RING - 1 < chunks)
        def _():
            fetch(chunk + RING - 1).start()

        fetch(chunk).wait()
        slot = lax.rem(chunk, RING)
        for at in range(CHUNK):
            k = chunk * CHUNK + at
            col = jnp.where(k < count, cols_ref[k], col_tiles)
            part = dot(buffer_ref[slot, at], received_ref[rows_ref[k]], 0, 0)
            sums_ref[col] += part
        return carry

    lax.fori_loop(0, chunks, step, 0)
    out_ref[...] = sums_ref[:col_tiles].astype(BF16)


def finish_kernel(parts_ref, feats_ref, weight_ref, second_ref, hidden_ref, send_ref):
    sources = parts_ref.shape[0]
    total = parts_ref[0].astype(F32)
    for source in range(1, sources):
        total = total + parts_ref[source].astype(F32)
    grad_hidden = total.astype(BF16)
    hidden_ref[...] = grad_hidden
    feats = feats_ref[...]
    pre = dot(feats, weight_ref[...], 1, 0)
    sig = sigmoid(pre)
    slope = sig * (1.0 + pre * (1.0 - sig))
    dpre = (grad_hidden.astype(F32) * slope).astype(BF16)
    first = dot(feats, dpre, 0, 0)
    features = first.shape[0]
    lanes = send_ref.shape[2]
    halves = features // lanes
    block = send_ref.shape[1]
    per_grad = features // block * halves
    for which, grad in enumerate((first, second_ref[...])):
        for half in range(halves):
            piece = grad[:, half * lanes : (half + 1) * lanes].astype(BF16)
            piece = piece.reshape(features // block, block, lanes)
            for row in range(features // block):
                send_ref[which * per_grad + row * halves + half] = piece[row]


def on_device(
    feats_one,
    feats_two,
    target_view,
    negatives,
    weight_one,
    weight_two,
    block_tiles,
    tile_rows,
    tile_cols,
    block_counts,
    need_rows,
):
    node_dev, features = feats_two.shape
    tile_size = block_tiles.shape[1]
    sources = lax.axis_size("col")
    row_group = lax.axis_size("row")
    devices = sources * row_group
    tiles_dev = node_dev // tile_size
    slot_count = need_rows.shape[2]
    col_count = row_group * tiles_dev
    row_slots = sources * slot_count
    weight_norm = 1.0 / math.sqrt(node_dev * devices)
    vmem = pl.BlockSpec(memory_space=pltpu.VMEM)
    smem = pl.BlockSpec(memory_space=pltpu.SMEM)

    wanted = lax.all_to_all(need_rows[0], "col", 0, 0, tiled=True)
    send, second = pl.pallas_call(
        message_kernel,
        out_shape=(
            jax.ShapeDtypeStruct((row_slots, tile_size, features), BF16),
            jax.ShapeDtypeStruct((features, features), F32),
        ),
        in_specs=[smem, vmem, vmem, vmem, vmem],
        out_specs=(vmem, vmem),
        scratch_shapes=[pltpu.VMEM((tiles_dev, tile_size, features), BF16)],
        name="message",
    )(wanted.reshape(row_slots), feats_two, target_view, negatives.reshape(1, node_dev), weight_two)
    received = lax.all_to_all(
        send.reshape(sources, slot_count * tile_size, features), "col", 0, 0, tiled=True
    ).reshape(row_slots, tile_size, features)
    partial = pl.pallas_call(
        product_kernel,
        out_shape=jax.ShapeDtypeStruct((col_count, tile_size, features), BF16),
        in_specs=[smem, smem, smem, pl.BlockSpec(memory_space=pl.ANY), vmem],
        out_specs=vmem,
        scratch_shapes=[
            pltpu.VMEM((col_count + 1, tile_size, features), F32),
            pltpu.VMEM((RING, CHUNK, tile_size, tile_size), BF16),
            pltpu.SemaphoreType.DMA((RING,)),
        ],
        name="product",
    )(tile_rows, tile_cols, block_counts, block_tiles, received)
    parts = lax.all_to_all(
        partial.reshape(row_group, node_dev, features), "row", 0, 0, tiled=True
    )
    lanes = 128
    block = 2 * features * features // (devices * lanes)
    grad_hidden, grads = pl.pallas_call(
        finish_kernel,
        out_shape=(
            jax.ShapeDtypeStruct((node_dev, features), BF16),
            jax.ShapeDtypeStruct((devices, block, lanes), BF16),
        ),
        in_specs=[vmem] * 4,
        out_specs=(vmem, vmem),
        name="finish",
    )(parts, feats_one, weight_one, second)
    pieces = lax.all_to_all(grads, ("row", "col"), 0, 0, tiled=True)
    mine = jnp.sum(pieces.astype(F32), axis=0, keepdims=True) * weight_norm
    whole = lax.all_to_all(
        jnp.broadcast_to(mine, (devices, block, lanes)), ("row", "col"), 0, 0, tiled=True
    )
    whole = whole.reshape(2, features // block, features // lanes, block, lanes)
    whole = whole.transpose(0, 1, 3, 2, 4).reshape(2, features, features)
    return (grad_hidden, whole[0], whole[1])


def solution(mesh):
    return jax.shard_map(
        on_device,
        mesh=mesh,
        in_specs=(
            P(("row", "col"), None),
            P(("row", "col"), None),
            P(("row", "col"), None),
            P(("row", "col")),
            P(),
            P(),
            P(("row", "col"), None, None),
            P(("row", "col")),
            P(("row", "col")),
            P(("row", "col")),
            P(("row", "col"), None, None),
        ),
        out_specs=(P(("row", "col"), None), P(), P()),
        check_vma=False,
    )
```

time: 546 us -> 141 us (0.26)
  waiting for transfers between devices: 228 us -> 27.9 us
  matrix products: 198 us -> 0 us
  local copies, waits for them, and re-layouts: 95.4 us -> 4.03 us
  blocking collectives: 0 us -> 84.4 us
  Pallas kernels: 0 us -> 18.5 us
  between operations: 14.6 us -> 1.31 us
  other arithmetic: 7.94 us -> 0.81 us
    dot_general x14 -> x0, matrix products: 198 us -> none  [the longest x5 130 us: add_block(): jnp.einsum('kc,kuf->cuf', selector, contrib, precision=lax.Precision.HIGH...]
    psum x1 -> x0, waiting for transfers between devices: 147 us -> none  [on_device(): grad_first = lax.psum(grad_first, ('row', 'col'))]
    all_to_all x0 -> x4, blocking collectives: none -> 84.4 us  [the longest x1 31 us: on_device(): lax.all_to_all(partial.reshape(row_group, node_dev, features), 'row', 0,...]
    reduce_scatter x1 -> x0, waiting for transfers between devices: 50.9 us -> none  [on_device(): lax.psum_scatter(summed_tiles.reshape(col_count * tile_size, features), '...]
    gather x7 -> x0, local copies, waits for them, and re-layouts: 45.5 us -> none  [the longest x5 43.7 us: add_block(): gathered_rows = buffer_tiles[row_part]]
    unnamed x23 -> x2, local copies, waits for them, and re-layouts: 39.7 us -> 1.31 us
    all_gather x1 -> x0, waiting for transfers between devices: 30.8 us -> none  [on_device(): gathered = lax.all_gather(message, 'col', axis=0, tiled=True)]
    all_to_all x0 -> x1, waiting for transfers between devices: none -> 27.9 us  [on_device(): lax.all_to_all(send.reshape(sources, slot_count * tile_size, features), '...]
  transfers between devices with their start and end apart: 3 -> 1, of which waited for: 3 -> 1; matrix products, arithmetic and copies ran while one was open for 6% -> 0% of each run, Pallas kernels for 0% -> 0%
where the time goes in v1:
time: 141 us
  blocking collectives  84.4 us (60%)
  waiting for transfers between devices  27.9 us (20%)
  Pallas kernels  18.5 us (13%)
  starting transfers between devices  4.17 us (3%)
  local copies, waits for them, and re-layouts  4.03 us (3%)
    all_to_all x1, blocking collectives, on_device(): lax.all_to_all(partial.reshape(row_group, node_dev, features), 'row', 0,...  31 us
    all_to_all x1, waiting for transfers between devices, on_device(): lax.all_to_all(send.reshape(sources, slot_count * tile_size, features), '...  27.9 us
    all_to_all x1, blocking collectives, on_device(): pieces = lax.all_to_all(grads, ('row', 'col'), 0, 0, tiled=True)  20.8 us
    all_to_all x1, blocking collectives, on_device(): lax.all_to_all(jnp.broadcast_to(mine, (devices, block, lanes)), ('row', '...  17.4 us
    all_to_all x1, blocking collectives, on_device(): wanted = lax.all_to_all(need_rows[0], 'col', 0, 0, tiled=True)  15.2 us
    pallas_call x1, Pallas kernels, on_device(): pl.pallas_call(product_kernel, out_shape=jax.ShapeDtypeStruct((col_count,...  10.9 us
    pallas_call x1, Pallas kernels, on_device(): pl.pallas_call(message_kernel, out_shape=(jax.ShapeDtypeStruct((row_slots...  4.47 us
    all_to_all x1, starting transfers between devices, on_device(): lax.all_to_all(send.reshape(sources, slot_count * tile_size, features), '...  4.17 us
  transfers between devices with their start and end apart: 1, of which 1 were waited for; matrix products, arithmetic and copies ran while one was open for 0% of the time, Pallas kernels for 0%

profile of v1, /device:TPU:1, one launch (start us, length us, event | category | flops | bytes accessed | tf_op | source)
XLA Modules:
  0.0 141.1 jit_solution(10000467337558942925)
XLA Ops:
  0.6 0.8 copy.16
  1.4 15.2 %all_to_all.29 = s32[16,1,2]{2,1,0:T(1,128)S(1)} all-to-all(s32[16,1,2]{2,1,0:T(1,128)S(1)} %copy.16), channel_id=1, replica_groups=mesh['row'=8,'col'=16] {'col'}, dimensions={0} | all-to-all | bytes 256 | tf_op jit(solution)/shard_map/all_to_all | solution.py:154
  16.6 0.5 broadcast.8
  17.1 0.7 reduce.3
  17.8 0.6 reshape.37.need_ref
  18.4 4.5 %message.1 = (bf16[32,128,256]{2,1,0:T(8,128)(2,1)}, f32[256,256]{1,0:T(8,128)}) custom-call(s32[32]{0:T(128)} %reshape.37.need_ref, bf16[512,256]{1,0:T(8,128)(2,1)} %feats_ref.2, bf16[512,256]{1,0:T(8,128)(2,1)} %target_ref.1, s32[1,512]{1,0:T(1,128)} %bitcast.16, bf16[256,256]{1,0:T(8,128)(2,1)} %weight_ref.2), custom_call_target="tpu_custom_call" | custom-call | tf_op jit(solution)/shard_map/message/pallas_call | solution.py:155
  22.9 4.2 %all-to-all-start.1 = ((bf16[16,256,256]{2,1,0:T(8,128)(2,1)}), bf16[16,256,256]{2,1,0:T(8,128)(2,1)S(1)}, u32[]{:S(2)}, u32[]{:S(2)}) async-start(bf16[16,256,256]{2,1,0:T(8,128)(2,1)} %bitcast.14), calls=%async_computation.1 | async-start | bytes 4194304 | tf_op jit(solution)/shard_map/all_to_all | solution.py:166
  27.7 27.9 %all-to-all-done.1 = bf16[16,256,256]{2,1,0:T(8,128)(2,1)S(1)} async-done(((bf16[16,256,256]{2,1,0:T(8,128)(2,1)}), bf16[16,256,256]{2,1,0:T(8,128)(2,1)S(1)}, u32[]{:S(2)}, u32[]{:S(2)}) %all-to-all-start.1) | async-done | bytes 2097184 | tf_op jit(solution)/shard_map/all_to_all | solution.py:166
  55.6 0.0 copy-start
  55.6 1.3 copy-done
  56.9 10.9 %product.1 = bf16[32,128,256]{2,1,0:T(8,128)(2,1)} custom-call(s32[640]{0:T(1024)} %rows_ref.1, s32[640]{0:T(1024)} %cols_ref.1, s32[1]{0:T(128)S(6)} %copy.17.count_ref, bf16[640,128,128]{2,1,0:T(8,128)(2,1)} %tiles_ref.1, bf16[32,128,256]{2,1,0:T(8,128)(2,1)} %bitcast.12), custom_call_target="tpu_custom_call" | custom-call | tf_op jit(solution)/shard_map/product/pallas_call | solution.py:169
  67.8 31.0 %all_to_all.30.parts_ref = bf16[8,512,256]{2,1,0:T(8,128)(2,1)} all-to-all(bf16[8,512,256]{2,1,0:T(8,128)(2,1)} %bitcast.13), channel_id=1, replica_groups=mesh['row'=8,'col'=16] {'row'}, dimensions={0} | all-to-all | bytes 4194304 | tf_op jit(solution)/shard_map/all_to_all | solution.py:181
  98.7 3.1 %finish.1 = (bf16[512,256]{1,0:T(8,128)(2,1)}, bf16[128,8,128]{2,1,0:T(8,128)(2,1)}) custom-call(bf16[8,512,256]{2,1,0:T(8,128)(2,1)} %all_to_all.30.parts_ref, bf16[512,256]{1,0:T(8,128)(2,1)} %feats_ref.3, bf16[256,256]{1,0:T(8,128)(2,1)} %weight_ref.3, f32[256,256]{1,0:T(8,128)} %get-tuple-element.8.second_ref), custom_call_target="tpu_custom_call" | custom-call | tf_op jit(solution)/shard_map/finish/pallas_call | solution.py:186
  101.9 20.8 %all_to_all.31 = bf16[128,8,128]{2,1,0:T(8,128)(2,1)S(1)} all-to-all(bf16[128,8,128]{2,1,0:T(8,128)(2,1)} %get-tuple-element.10), channel_id=1, replica_groups=mesh['row'=8,'col'=16] {'row','col'}, dimensions={0} | all-to-all | bytes 524288 | tf_op jit(solution)/shard_map/all_to_all | solution.py:196
  122.6 0.1 convert_reduce_fusion
  122.8 17.4 %all_to_all.32 = f32[128,8,128]{2,1,0:T(8,128)S(1)} all-to-all(f32[128,8,128]{2,1,0:T(8,128)S(1)} %broadcast_in_dim.2), channel_id=1, replica_groups=mesh['row'=8,'col'=16] {'row','col'}, dimensions={0} | all-to-all | bytes 1048576 | tf_op jit(solution)/shard_map/all_to_all | solution.py:198
  140.2 0.8 slice_bitcast_fusion
  (2 shorter events, 0.0 us)
Async XLA Ops:
  22.9 32.7 %all-to-all-start.1 = ((bf16[16,256,256]{2,1,0:T(8,128)(2,1)}), bf16[16,256,256]{2,1,0:T(8,128)(2,1)S(1)}, u32[]{:S(2)}, u32[]{:S(2)}) async-start(bf16[16,256,256]{2,1,0:T(8,128)(2,1)} %bitcast.14), calls=%async_computation.1 | async-start | bytes 4194304 | tf_op jit(solution)/shard_map/all_to_all | solution.py:166
  55.6 1.3 copy-start

commit v2 on v1

--- a/solution.py
+++ b/solution.py
@@ -30,10 +30,10 @@
 
 
 def message_kernel(
-    need_ref, feats_ref, target_ref, negatives_ref, weight_ref, send_ref, grad_ref, message_ref
+    feats_ref, target_ref, negatives_ref, weight_ref, message_ref, grad_ref
 ):
     nodes, features = feats_ref.shape
-    tiles, tile_size, _ = message_ref.shape
+    tiles, _, tile_size = message_ref.shape
     inverse_root = 1.0 / math.sqrt(features)
     feats = feats_ref[...]
     weight = weight_ref[...]
@@ -52,10 +52,13 @@
     both = dot(picks, split(prob_neg * hidden), 1, 0)
     grad_out = prob_neg * partner - prob_pos * target + both[:, :features] + both[:, features:]
     dpre = (grad_out * (sig * (1.0 + pre * (1.0 - sig)))).astype(BF16)
-    message = dot(dpre, weight, 1, 1).astype(BF16)
-    message_ref[...] = message.reshape(tiles, tile_size, features)
+    message = dot(weight, dpre, 1, 1).astype(BF16)
+    for tile in range(tiles):
+        message_ref[tile] = message[:, tile * tile_size : (tile + 1) * tile_size]
     grad_ref[...] = dot(feats, dpre, 0, 0)
 
+
+def select_kernel(need_ref, message_ref, send_ref):
     for slot in range(send_ref.shape[0]):
         send_ref[slot] = message_ref[need_ref[slot]]
 
@@ -91,7 +94,7 @@
         for at in range(CHUNK):
             k = chunk * CHUNK + at
             col = jnp.where(k < count, cols_ref[k], col_tiles)
-            part = dot(buffer_ref[slot, at], received_ref[rows_ref[k]], 0, 0)
+            part = dot(received_ref[rows_ref[k]], buffer_ref[slot, at], 1, 0)
             sums_ref[col] += part
         return carry
 
@@ -104,7 +107,9 @@
     total = parts_ref[0].astype(F32)
     for source in range(1, sources):
         total = total + parts_ref[source].astype(F32)
-    grad_hidden = total.astype(BF16)
+    grad_hidden = jnp.concatenate(
+        [total[tile].T for tile in range(total.shape[0])], axis=0
+    ).astype(BF16)
     hidden_ref[...] = grad_hidden
     feats = feats_ref[...]
     pre = dot(feats, weight_ref[...], 1, 0)
@@ -152,35 +157,41 @@
     smem = pl.BlockSpec(memory_space=pltpu.SMEM)
 
     wanted = lax.all_to_all(need_rows[0], "col", 0, 0, tiled=True)
-    send, second = pl.pallas_call(
+    message, second = pl.pallas_call(
         message_kernel,
         out_shape=(
-            jax.ShapeDtypeStruct((row_slots, tile_size, features), BF16),
+            jax.ShapeDtypeStruct((tiles_dev, features, tile_size), BF16),
             jax.ShapeDtypeStruct((features, features), F32),
         ),
-        in_specs=[smem, vmem, vmem, vmem, vmem],
+        in_specs=[vmem] * 4,
         out_specs=(vmem, vmem),
-        scratch_shapes=[pltpu.VMEM((tiles_dev, tile_size, features), BF16)],
         name="message",
-    )(wanted.reshape(row_slots), feats_two, target_view, negatives.reshape(1, node_dev), weight_two)
+    )(feats_two, target_view, negatives.reshape(1, node_dev), weight_two)
+    send = pl.pallas_call(
+        select_kernel,
+        out_shape=jax.ShapeDtypeStruct((row_slots, features, tile_size), BF16),
+        in_specs=[smem, vmem],
+        out_specs=vmem,
+        name="select",
+    )(wanted.reshape(row_slots), message)
     received = lax.all_to_all(
-        send.reshape(sources, slot_count * tile_size, features), "col", 0, 0, tiled=True
-    ).reshape(row_slots, tile_size, features)
+        send.reshape(sources, slot_count * features, tile_size), "col", 0, 0, tiled=True
+    ).reshape(row_slots, features, tile_size)
     partial = pl.pallas_call(
         product_kernel,
-        out_shape=jax.ShapeDtypeStruct((col_count, tile_size, features), BF16),
+        out_shape=jax.ShapeDtypeStruct((col_count, features, tile_size), BF16),
         in_specs=[smem, smem, smem, pl.BlockSpec(memory_space=pl.ANY), vmem],
         out_specs=vmem,
         scratch_shapes=[
-            pltpu.VMEM((col_count + 1, tile_size, features), F32),
+            pltpu.VMEM((col_count + 1, features, tile_size), F32),
             pltpu.VMEM((RING, CHUNK, tile_size, tile_size), BF16),
             pltpu.SemaphoreType.DMA((RING,)),
         ],
         name="product",
     )(tile_rows, tile_cols, block_counts, block_tiles, received)
     parts = lax.all_to_all(
-        partial.reshape(row_group, node_dev, features), "row", 0, 0, tiled=True
-    )
+        partial.reshape(row_group, tiles_dev * features, tile_size), "row", 0, 0, tiled=True
+    ).reshape(row_group, tiles_dev, features, tile_size)
     lanes = 128
     block = 2 * features * features // (devices * lanes)
     grad_hidden, grads = pl.pallas_call(

time: 141 us -> 139 us (0.986)
  blocking collectives: 84.4 us -> 69.1 us
  starting transfers between devices: 4.17 us -> 12.6 us
  waiting for transfers between devices: 27.9 us -> 31 us
    all_to_all x2 -> x1, blocking collectives: 46.2 us -> 33.1 us  [on_device(): lax.all_to_all(partial.reshape(row_group, tiles_dev * features, tile_size...]
    all_to_all x1 -> x2, starting transfers between devices: 4.17 us -> 12.6 us  [the longest x1 8.45 us: on_device(): wanted = lax.all_to_all(need_rows[0], 'col', 0, 0, tiled=True)]
    all_to_all x1 -> x2, waiting for transfers between devices: 27.9 us -> 31 us  [the longest x1 27.9 us: on_device(): lax.all_to_all(send.reshape(sources, slot_count * features, tile_size), '...]
    all_to_all x1, blocking collectives: 20.8 us -> 18.5 us  [on_device(): pieces = lax.all_to_all(grads, ('row', 'col'), 0, 0, tiled=True)]
    pallas_call x1 -> x2, Pallas kernels: 4.47 us -> 6.19 us  [the longest x1 3.75 us: on_device(): pl.pallas_call(message_kernel, out_shape=(jax.ShapeDtypeStruct((tiles_dev...]
  transfers between devices with their start and end apart: 1 -> 2, of which waited for: 1 -> 2; matrix products, arithmetic and copies ran while one was open for 0% -> 0% of each run, Pallas kernels for 0% -> 3%
where the time goes in v2:
time: 139 us
  blocking collectives  69.1 us (50%)
  waiting for transfers between devices  31 us (22%)
  Pallas kernels  19.2 us (14%)
  starting transfers between devices  12.6 us (9%)
  local copies, waits for them, and re-layouts  4.63 us (3%)
    all_to_all x1, blocking collectives, on_device(): lax.all_to_all(partial.reshape(row_group, tiles_dev * features, tile_size...  33.1 us
    all_to_all x1, waiting for transfers between devices, on_device(): lax.all_to_all(send.reshape(sources, slot_count * features, tile_size), '...  27.9 us
    all_to_all x1, blocking collectives, on_device(): pieces = lax.all_to_all(grads, ('row', 'col'), 0, 0, tiled=True)  18.5 us
    all_to_all x1, blocking collectives, on_device(): lax.all_to_all(jnp.broadcast_to(mine, (devices, block, lanes)), ('row', '...  17.4 us
    pallas_call x1, Pallas kernels, on_device(): pl.pallas_call(product_kernel, out_shape=jax.ShapeDtypeStruct((col_count,...  9.92 us
    all_to_all x1, starting transfers between devices, on_device(): wanted = lax.all_to_all(need_rows[0], 'col', 0, 0, tiled=True)  8.45 us
    all_to_all x1, starting transfers between devices, on_device(): lax.all_to_all(send.reshape(sources, slot_count * features, tile_size), '...  4.17 us
    pallas_call x1, Pallas kernels, on_device(): pl.pallas_call(message_kernel, out_shape=(jax.ShapeDtypeStruct((tiles_dev...  3.75 us
  transfers between devices with their start and end apart: 2, of which 2 were waited for; matrix products, arithmetic and copies ran while one was open for 0% of the time, Pallas kernels for 3%

profile of v2, /device:TPU:1, one launch (start us, length us, event | category | flops | bytes accessed | tf_op | source)
XLA Modules:
  0.0 138.6 jit_solution(10468841442393304777)
XLA Ops:
  0.6 1.4 copy.16
  2.0 8.4 %all-to-all-start = ((s32[16,1,2]{2,1,0:T(1,128)}), s32[16,1,2]{2,1,0:T(1,128)S(1)}, u32[]{:S(2)}, u32[]{:S(2)}) async-start(s32[16,1,2]{2,1,0:T(1,128)} %copy.16), calls=%async_computation | async-start | bytes 16384 | tf_op jit(solution)/shard_map/all_to_all | solution.py:159
  10.4 3.8 %message.1 = (bf16[4,256,128]{2,1,0:T(8,128)(2,1)}, f32[256,256]{1,0:T(8,128)}) custom-call(bf16[512,256]{1,0:T(8,128)(2,1)} %feats_ref.2, bf16[512,256]{1,0:T(8,128)(2,1)} %target_ref.1, s32[1,512]{1,0:T(1,128)} %bitcast.18, bf16[256,256]{1,0:T(8,128)(2,1)} %weight_ref.2), custom_call_target="tpu_custom_call" | custom-call | tf_op jit(solution)/shard_map/message/pallas_call | solution.py:160
  14.2 3.2 %all-to-all-done = s32[16,1,2]{2,1,0:T(1,128)S(1)} async-done(((s32[16,1,2]{2,1,0:T(1,128)}), s32[16,1,2]{2,1,0:T(1,128)S(1)}, u32[]{:S(2)}, u32[]{:S(2)}) %all-to-all-start) | async-done | bytes 160 | tf_op jit(solution)/shard_map/all_to_all | solution.py:159
  17.3 0.5 broadcast.8
  17.9 0.7 reduce.3
  18.5 0.6 reshape.40.need_ref
  19.1 2.4 %select.1 = bf16[32,256,128]{2,1,0:T(8,128)(2,1)} custom-call(s32[32]{0:T(128)} %reshape.40.need_ref, bf16[4,256,128]{2,1,0:T(8,128)(2,1)} %get-tuple-element.7.message_ref), custom_call_target="tpu_custom_call" | custom-call | tf_op jit(solution)/shard_map/select/pallas_call | solution.py:170
  21.6 4.2 %all-to-all-start.1 = ((bf16[16,512,128]{2,1,0:T(8,128)(2,1)}), bf16[16,512,128]{2,1,0:T(8,128)(2,1)S(1)}, u32[]{:S(2)}, u32[]{:S(2)}) async-start(bf16[16,512,128]{2,1,0:T(8,128)(2,1)} %bitcast.15), calls=%async_computation.1 | async-start | bytes 4194304 | tf_op jit(solution)/shard_map/all_to_all | solution.py:177
  26.4 27.9 %all-to-all-done.1 = bf16[16,512,128]{2,1,0:T(8,128)(2,1)S(1)} async-done(((bf16[16,512,128]{2,1,0:T(8,128)(2,1)}), bf16[16,512,128]{2,1,0:T(8,128)(2,1)S(1)}, u32[]{:S(2)}, u32[]{:S(2)}) %all-to-all-start.1) | async-done | bytes 2097184 | tf_op jit(solution)/shard_map/all_to_all | solution.py:177
  54.3 0.0 copy-start
  54.3 1.3 copy-done
  55.6 9.9 %product.1 = bf16[32,256,128]{2,1,0:T(8,128)(2,1)} custom-call(s32[640]{0:T(1024)} %rows_ref.1, s32[640]{0:T(1024)} %cols_ref.1, s32[1]{0:T(128)S(6)} %copy.17.count_ref, bf16[640,128,128]{2,1,0:T(8,128)(2,1)} %tiles_ref.1, bf16[32,256,128]{2,1,0:T(8,128)(2,1)} %bitcast.13), custom_call_target="tpu_custom_call" | custom-call | tf_op jit(solution)/shard_map/product/pallas_call | solution.py:180
  65.5 33.1 %all_to_all.29 = bf16[8,1024,128]{2,1,0:T(8,128)(2,1)} all-to-all(bf16[8,1024,128]{2,1,0:T(8,128)(2,1)} %bitcast.14), channel_id=1, replica_groups=mesh['row'=8,'col'=16] {'row'}, dimensions={0} | all-to-all | bytes 4194304 | tf_op jit(solution)/shard_map/all_to_all | solution.py:192
  98.6 3.1 %finish.1 = (bf16[512,256]{1,0:T(8,128)(2,1)}, bf16[128,8,128]{2,1,0:T(8,128)(2,1)}) custom-call(bf16[8,4,256,128]{3,2,1,0:T(8,128)(2,1)} %bitcast.16, bf16[512,256]{1,0:T(8,128)(2,1)} %feats_ref.3, bf16[256,256]{1,0:T(8,128)(2,1)} %weight_ref.3, f32[256,256]{1,0:T(8,128)} %get-tuple-element.8.second_ref), custom_call_target="tpu_custom_call" | custom-call | tf_op jit(solution)/shard_map/finish/pallas_call | solution.py:197
  101.7 18.5 %all_to_all.30 = bf16[128,8,128]{2,1,0:T(8,128)(2,1)S(1)} all-to-all(bf16[128,8,128]{2,1,0:T(8,128)(2,1)} %get-tuple-element.10), channel_id=1, replica_groups=mesh['row'=8,'col'=16] {'row','col'}, dimensions={0} | all-to-all | bytes 524288 | tf_op jit(solution)/shard_map/all_to_all | solution.py:207
  120.2 0.1 convert_reduce_fusion
  120.4 17.4 %all_to_all.31 = f32[128,8,128]{2,1,0:T(8,128)S(1)} all-to-all(f32[128,8,128]{2,1,0:T(8,128)S(1)} %broadcast_in_dim.2), channel_id=1, replica_groups=mesh['row'=8,'col'=16] {'row','col'}, dimensions={0} | all-to-all | bytes 1048576 | tf_op jit(solution)/shard_map/all_to_all | solution.py:209
  137.8 0.8 slice_bitcast_fusion
  (2 shorter events, 0.0 us)
Async XLA Ops:
  2.0 15.4 %all-to-all-start = ((s32[16,1,2]{2,1,0:T(1,128)}), s32[16,1,2]{2,1,0:T(1,128)S(1)}, u32[]{:S(2)}, u32[]{:S(2)}) async-start(s32[16,1,2]{2,1,0:T(1,128)} %copy.16), calls=%async_computation | async-start | bytes 16384 | tf_op jit(solution)/shard_map/all_to_all | solution.py:159
  21.6 32.7 %all-to-all-start.1 = ((bf16[16,512,128]{2,1,0:T(8,128)(2,1)}), bf16[16,512,128]{2,1,0:T(8,128)(2,1)S(1)}, u32[]{:S(2)}, u32[]{:S(2)}) async-start(bf16[16,512,128]{2,1,0:T(8,128)(2,1)} %bitcast.15), calls=%async_computation.1 | async-start | bytes 4194304 | tf_op jit(solution)/shard_map/all_to_all | solution.py:177
  54.3 1.3 copy-start

commit v3 on v2

--- a/solution.py
+++ b/solution.py
@@ -59,8 +59,9 @@
 
 
 def select_kernel(need_ref, message_ref, send_ref):
+    slots = need_ref.shape[1]
     for slot in range(send_ref.shape[0]):
-        send_ref[slot] = message_ref[need_ref[slot]]
+        send_ref[slot] = message_ref[need_ref[slot // slots, slot % slots]]
 
 
 def product_kernel(
@@ -173,7 +174,7 @@
         in_specs=[smem, vmem],
         out_specs=vmem,
         name="select",
-    )(wanted.reshape(row_slots), message)
+    )(wanted, message)
     received = lax.all_to_all(
         send.reshape(sources, slot_count * features, tile_size), "col", 0, 0, tiled=True
     ).reshape(row_slots, features, tile_size)
@@ -206,11 +207,12 @@
     )(parts, feats_one, weight_one, second)
     pieces = lax.all_to_all(grads, ("row", "col"), 0, 0, tiled=True)
     mine = jnp.sum(pieces.astype(F32), axis=0, keepdims=True) * weight_norm
+    mine = mine.astype(BF16)
     whole = lax.all_to_all(
         jnp.broadcast_to(mine, (devices, block, lanes)), ("row", "col"), 0, 0, tiled=True
     )
     whole = whole.reshape(2, features // block, features // lanes, block, lanes)
-    whole = whole.transpose(0, 1, 3, 2, 4).reshape(2, features, features)
+    whole = whole.transpose(0, 1, 3, 2, 4).reshape(2, features, features).astype(F32)
     return (grad_hidden, whole[0], whole[1])
 
 

time: 139 us -> 136 us (0.978)
  blocking collectives: 69.1 us -> 65 us
    all_to_all x1, blocking collectives: 17.4 us -> 14.9 us  [on_device(): lax.all_to_all(jnp.broadcast_to(mine, (devices, block, lanes)), ('row', '...]
    all_to_all x1, blocking collectives: 33.1 us -> 30.9 us  [on_device(): lax.all_to_all(partial.reshape(row_group, tiles_dev * features, tile_size...]
where the time goes in v3:
time: 136 us; the launch traced here: 134 us
  blocking collectives  65 us (48%)
  waiting for transfers between devices  31 us (23%)
  Pallas kernels  20.1 us (15%)
  starting transfers between devices  12.6 us (9%)
  local copies, waits for them, and re-layouts  4.13 us (3%)
    all_to_all x1, blocking collectives, on_device(): lax.all_to_all(partial.reshape(row_group, tiles_dev * features, tile_size...  30.9 us
    all_to_all x1, waiting for transfers between devices, on_device(): lax.all_to_all(send.reshape(sources, slot_count * features, tile_size), '...  27.9 us
    all_to_all x1, blocking collectives, on_device(): pieces = lax.all_to_all(grads, ('row', 'col'), 0, 0, tiled=True)  19.2 us
    all_to_all x1, blocking collectives, on_device(): lax.all_to_all(jnp.broadcast_to(mine, (devices, block, lanes)), ('row', '...  14.9 us
    pallas_call x1, Pallas kernels, on_device(): pl.pallas_call(product_kernel, out_shape=jax.ShapeDtypeStruct((col_count,...  10.8 us
    all_to_all x1, starting transfers between devices, on_device(): wanted = lax.all_to_all(need_rows[0], 'col', 0, 0, tiled=True)  8.45 us
    all_to_all x1, starting transfers between devices, on_device(): lax.all_to_all(send.reshape(sources, slot_count * features, tile_size), '...  4.17 us
    pallas_call x1, Pallas kernels, on_device(): pl.pallas_call(message_kernel, out_shape=(jax.ShapeDtypeStruct((tiles_dev...  3.75 us
  transfers between devices with their start and end apart: 2, of which 2 were waited for; matrix products, arithmetic and copies ran while one was open for 0% of the time, Pallas kernels for 3%

profile of v3, /device:TPU:1, one launch (start us, length us, event | category | flops | bytes accessed | tf_op | source)
XLA Modules:
  0.0 134.4 jit_solution(13489732225232622182)
XLA Ops:
  0.6 1.4 %copy.15 = s32[16,1,2]{2,1,0:T(1,128)} copy(s32[16,1,2]{0,2,1:T(2,128)} %bitcast.22) | data formatting | bytes 256 | tf_op jit(solution)/shard_map/all_to_all | solution.py:160
  2.0 8.4 %all-to-all-start = ((s32[16,1,2]{2,1,0:T(1,128)}), s32[16,1,2]{2,1,0:T(1,128)S(1)}, u32[]{:S(2)}, u32[]{:S(2)}) async-start(s32[16,1,2]{2,1,0:T(1,128)} %copy.15), calls=%async_computation | async-start | bytes 16384 | tf_op jit(solution)/shard_map/all_to_all | solution.py:160
  10.4 3.8 %message.1 = (bf16[4,256,128]{2,1,0:T(8,128)(2,1)}, f32[256,256]{1,0:T(8,128)}) custom-call(bf16[512,256]{1,0:T(8,128)(2,1)} %feats_ref.2, bf16[512,256]{1,0:T(8,128)(2,1)} %target_ref.1, s32[1,512]{1,0:T(1,128)} %bitcast.21, bf16[256,256]{1,0:T(8,128)(2,1)} %weight_ref.2), custom_call_target="tpu_custom_call" | custom-call | tf_op jit(solution)/shard_map/message/pallas_call | solution.py:161
  14.2 3.2 %all-to-all-done = s32[16,1,2]{2,1,0:T(1,128)S(1)} async-done(((s32[16,1,2]{2,1,0:T(1,128)}), s32[16,1,2]{2,1,0:T(1,128)S(1)}, u32[]{:S(2)}, u32[]{:S(2)}) %all-to-all-start) | async-done | bytes 160 | tf_op jit(solution)/shard_map/all_to_all | solution.py:160
  17.3 0.0 copy-start.1
  17.4 0.6 copy-done.1
  17.9 2.5 %select.1 = bf16[32,256,128]{2,1,0:T(8,128)(2,1)} custom-call(s32[16,2]{1,0:T(8,128)} %bitcast.20, bf16[4,256,128]{2,1,0:T(8,128)(2,1)} %get-tuple-element.7.message_ref), custom_call_target="tpu_custom_call" | custom-call | tf_op jit(solution)/shard_map/select/pallas_call | solution.py:171
  20.4 4.2 %all-to-all-start.1 = ((bf16[16,512,128]{2,1,0:T(8,128)(2,1)}), bf16[16,512,128]{2,1,0:T(8,128)(2,1)S(1)}, u32[]{:S(2)}, u32[]{:S(2)}) async-start(bf16[16,512,128]{2,1,0:T(8,128)(2,1)} %bitcast.17), calls=%async_computation.1 | async-start | bytes 4194304 | tf_op jit(solution)/shard_map/all_to_all | solution.py:178
  25.2 27.9 %all-to-all-done.1 = bf16[16,512,128]{2,1,0:T(8,128)(2,1)S(1)} async-done(((bf16[16,512,128]{2,1,0:T(8,128)(2,1)}), bf16[16,512,128]{2,1,0:T(8,128)(2,1)S(1)}, u32[]{:S(2)}, u32[]{:S(2)}) %all-to-all-start.1) | async-done | bytes 2097184 | tf_op jit(solution)/shard_map/all_to_all | solution.py:178
  53.1 0.0 copy-start
  53.1 1.3 copy-done
  54.4 10.8 %product.1 = bf16[32,256,128]{2,1,0:T(8,128)(2,1)} custom-call(s32[640]{0:T(1024)} %rows_ref.1, s32[640]{0:T(1024)} %cols_ref.1, s32[1]{0:T(128)S(6)} %copy.19.count_ref, bf16[640,128,128]{2,1,0:T(8,128)(2,1)} %tiles_ref.1, bf16[32,256,128]{2,1,0:T(8,128)(2,1)} %bitcast.15), custom_call_target="tpu_custom_call" | custom-call | tf_op jit(solution)/shard_map/product/pallas_call | solution.py:181
  65.2 30.9 %all_to_all.31 = bf16[8,1024,128]{2,1,0:T(8,128)(2,1)} all-to-all(bf16[8,1024,128]{2,1,0:T(8,128)(2,1)} %bitcast.16), channel_id=1, replica_groups=mesh['row'=8,'col'=16] {'row'}, dimensions={0} | all-to-all | bytes 4194304 | tf_op jit(solution)/shard_map/all_to_all | solution.py:193
  96.2 3.1 %finish.1 = (bf16[512,256]{1,0:T(8,128)(2,1)}, bf16[128,8,128]{2,1,0:T(8,128)(2,1)}) custom-call(bf16[8,4,256,128]{3,2,1,0:T(8,128)(2,1)} %bitcast.18, bf16[512,256]{1,0:T(8,128)(2,1)} %feats_ref.3, bf16[256,256]{1,0:T(8,128)(2,1)} %weight_ref.3, f32[256,256]{1,0:T(8,128)} %get-tuple-element.8.second_ref), custom_call_target="tpu_custom_call" | custom-call | tf_op jit(solution)/shard_map/finish/pallas_call | solution.py:198
  99.2 19.2 %all_to_all.32 = bf16[128,8,128]{2,1,0:T(8,128)(2,1)S(1)} all-to-all(bf16[128,8,128]{2,1,0:T(8,128)(2,1)} %get-tuple-element.10), channel_id=1, replica_groups=mesh['row'=8,'col'=16] {'row','col'}, dimensions={0} | all-to-all | bytes 524288 | tf_op jit(solution)/shard_map/all_to_all | solution.py:208
  118.5 0.1 convert_reduce_fusion
  118.7 14.9 %all_to_all.33 = bf16[128,8,128]{2,1,0:T(8,128)(2,1)S(1)} all-to-all(bf16[128,8,128]{2,1,0:T(8,128)(2,1)S(1)} %broadcast_in_dim.2), channel_id=1, replica_groups=mesh['row'=8,'col'=16] {'row','col'}, dimensions={0} | all-to-all | bytes 524288 | tf_op jit(solution)/shard_map/all_to_all | solution.py:211
  133.6 0.8 slice_bitcast_fusion
  (3 shorter events, 0.1 us)
Async XLA Ops:
  2.0 15.4 %all-to-all-start = ((s32[16,1,2]{2,1,0:T(1,128)}), s32[16,1,2]{2,1,0:T(1,128)S(1)}, u32[]{:S(2)}, u32[]{:S(2)}) async-start(s32[16,1,2]{2,1,0:T(1,128)} %copy.15), calls=%async_computation | async-start | bytes 16384 | tf_op jit(solution)/shard_map/all_to_all | solution.py:160
  17.3 0.6 copy-start.1
  20.4 32.7 %all-to-all-start.1 = ((bf16[16,512,128]{2,1,0:T(8,128)(2,1)}), bf16[16,512,128]{2,1,0:T(8,128)(2,1)S(1)}, u32[]{:S(2)}, u32[]{:S(2)}) async-start(bf16[16,512,128]{2,1,0:T(8,128)(2,1)} %bitcast.17), calls=%async_computation.1 | async-start | bytes 4194304 | tf_op jit(solution)/shard_map/all_to_all | solution.py:178
  53.1 1.3 copy-start
